TPU v7x, 32 devices: a whole 2x2x4 slice. The times are simulated.
32 devices in a mesh: view: 4 (over y, core), slab: 8 (over z, x).
Axes of the slice: x: 2, y: 2, z: 4, core: 2. Of those that a mesh axis runs over, the one named last changes fastest.
Arguments:
- estimate: float32 [2, 128, 128, 1024], P(None, 'slab', 'view'), may hold values from 0.2 to 5
- recorded: bfloat16 [2, 2, 128, 128, 1024], P(None, None, None, 'view', 'slab'), may hold values from 0.19921875 to 5
- psf_lateral: float32 [2, 2, 31], replicated, may hold values from 0.0007 to 1.5, as said below
- psf_axial: float32 [2, 127], replicated, may hold values from 0.0007 to 1.5, as said below
- offsets: int32 [2, 2], replicated, may hold values from -8 to 8, as said below
Outputs:
- updated: float32 [2, 128, 128, 1024], P(None, 'slab', 'view')
Inputs may be any that keep to these rules, and one draw needn't show every extreme that they name: offsets[v] is imaging direction v's voxel shift along x and along y; the magnitude 8 occurs with both signs. `psf_lateral`: positive lateral taps. `psf_axial`: positive axial taps.
All inputs are finite; a program needn't handle non-finite values.
Results may differ from a plain program's by a relative error of at most 0.0003.
Values sent between devices are 32-bit elements; how exact they have to be, the bound alone decides.
No kernel may reach another device: no remote copies, remote signals or barrier semaphores. Data moves between devices by JAX's collectives and lax.ppermute only.
A program may use at most 128 MiB of HBM per device.

v0:
```python
import jax
import jax.numpy as jnp
from jax import lax
from jax.sharding import PartitionSpec as P

Z = 128
YBLK = 128
HALO = 23
BACKGROUND = 0.05
HIGHEST = lax.Precision.HIGHEST


def with_halo(value, sides, width):
    for axis, dim in sides:
        peers, length = (lax.axis_size(axis), value.shape[dim])
        up = [(i, (i + 1) % peers) for i in range(peers - 1)]
        down = [(j, i) for i, j in up]
        last = lax.slice_in_dim(value, length - width, length, axis=dim)
        leading = lax.slice_in_dim(value, 0, width, axis=dim)
        before = lax.ppermute(last, axis, up)
        after = lax.ppermute(leading, axis, down)
        value = jnp.concatenate([before, value, after], axis=dim)
    return value


def unit_taps(weights):
    return weights / jnp.sum(weights)


def band_table(weights, places):
    levels = jnp.arange(weights.shape[0], dtype=jnp.int32)
    return jnp.sum(jnp.where(places[..., None] == levels, weights, 0.0), axis=-1)


def margin_matrix(weights, offset, length, margin, adjoint):
    centre = (weights.shape[0] - 1) // 2
    outputs = jnp.arange(length, dtype=jnp.int32)[:, None]
    sources = jnp.arange(length + 2 * margin, dtype=jnp.int32)[None, :] - margin
    apart = sources - outputs
    if adjoint:
        apart = -apart
    return band_table(weights, apart - offset + centre)


def blocked_rows(field, weights, offset, width_blk, adjoint):
    extent = field.shape
    blocks = extent[3] // width_blk
    pieces = field.reshape(extent[0], extent[1], extent[2], blocks, width_blk)
    padded = jnp.pad(pieces, ((0, 0), (0, 0), (0, 0), (1, 1), (0, 0)))
    centre = (weights.shape[0] - 1) // 2
    sources = jnp.arange(width_blk, dtype=jnp.int32)[:, None]
    outputs = jnp.arange(width_blk, dtype=jnp.int32)[None, :]
    result = jnp.zeros(pieces.shape, jnp.float32)
    for shifted in range(3):
        apart = (shifted - 1) * width_blk + sources - outputs
        if adjoint:
            apart = -apart
        matrix = band_table(weights, apart - offset + centre)
        result = result + jnp.einsum(
            "czxkj,ji->czxki",
            padded[:, :, :, shifted : shifted + blocks],
            matrix,
            precision=HIGHEST,
        )
    return result.reshape(extent)


def shards(estimate, recorded, psf_lateral, psf_axial, offsets):
    views_n = recorded.shape[0]
    along_x = [unit_taps(psf_lateral[which, 0]) for which in range(views_n)]
    along_y = [unit_taps(psf_lateral[which, 1]) for which in range(views_n)]
    rows_at = jnp.arange(Z, dtype=jnp.int32)[:, None]
    cols_at = jnp.arange(Z, dtype=jnp.int32)[None, :]
    axial_places = cols_at - rows_at + (psf_axial.shape[1] - 1) // 2
    axial = [band_table(unit_taps(psf_axial[which]), axial_places) for which in range(views_n)]
    x_rows = estimate.shape[2]
    widened = with_halo(estimate, (("view", 2),), HALO)
    blurred = []
    for which in range(views_n):
        across = margin_matrix(along_x[which], offsets[which, 0], x_rows, HALO, False)
        sectioned = jnp.einsum("ab,czby->czay", across, widened, precision=HIGHEST)
        blurred.append(blocked_rows(sectioned, along_y[which], offsets[which, 1], YBLK, False))
    columns = lax.all_to_all(jnp.stack(blurred), "slab", split_axis=4, concat_axis=2, tiled=True)
    spread = []
    for which in range(views_n):
        imaged = jnp.einsum("oi,cixy->coxy", axial[which], columns[which], precision=HIGHEST)
        quotient = recorded[which].astype(jnp.float32) / (imaged + BACKGROUND)
        spread.append(jnp.einsum("oi,coxy->cixy", axial[which], quotient, precision=HIGHEST))
    planes = lax.all_to_all(jnp.stack(spread), "slab", split_axis=2, concat_axis=4, tiled=True)
    returned = [
        blocked_rows(planes[which], along_y[which], offsets[which, 1], YBLK, True)
        for which in range(views_n)
    ]
    fringe = with_halo(jnp.stack(returned), (("view", 3),), HALO)
    summed = jnp.zeros(estimate.shape, jnp.float32)
    for which in range(views_n):
        across = margin_matrix(along_x[which], offsets[which, 0], x_rows, HALO, True)
        summed = summed + jnp.einsum("ab,czby->czay", across, fringe[which], precision=HIGHEST)
    return estimate * (summed / views_n)


def solution(mesh):
    in_specs = (P(None, "slab", "view", None), P(None, None, None, "view", "slab"), P(), P(), P())
    out_specs = P(None, "slab", "view", None)
    return jax.shard_map(shards, mesh=mesh, in_specs=in_specs, out_specs=out_specs, check_vma=False)
```

profile of v0, /device:TPU:1, one launch (start us, length us, event | category | flops | bytes accessed | tf_op | source)
XLA Modules:
  0.0 831.5 jit_solution(896550517628313579)
XLA Ops:
  30.3 12.5 %collective-permute-done = f32[2,16,23,1024]{3,1,2,0:T(8,128)S(1)} collective-permute-done((f32[2,16,23,1024]{3,1,2,0:T(8,128)S(1)}, f32[2,16,23,1024]{3,1,2,0:T(8,128)S(1)}, u32[]{:S(2)}, u32[]{:S(2)}) %collective-permute-start) | collective-permute-done | bytes 3014688 | tf_op jit(solution)/shard_map/ppermute | solution.py:20
  50.7 11.1 %fusion.3 = f32[2,16,1024,32]{2,3,1,0:T(8,128)S(1)} fusion(f32[2,16,23,1024]{3,2,1,0:T(8,128)S(1)} %copy.64, f32[2,16,32,1024]{3,2,1,0:T(8,128)S(1)} %copy-done, f32[2,16,23,1024]{3,2,1,0:T(8,128)S(1)} %copy.63, f32[32,78]{1,0:T(8,128)S(1)} %get-tuple-element.61), kind=kOutput, calls=%fused_computation.21 | convolution fusion | flops 986578944 | bytes 14427904 | tf_op jit(solution)/shard_map/ab,czby->czay/dot_general | solution.py:81
  79.9 13.7 %fusion.2 = f32[2,16,1024,32]{2,3,1,0:T(8,128)S(1)} fusion(f32[2,16,23,1024]{3,2,1,0:T(8,128)} %copy-done.4, f32[2,16,32,1024]{3,2,1,0:T(8,128)} %param.5, f32[2,16,23,1024]{3,2,1,0:T(8,128)S(1)} %copy.63, f32[32,78]{1,0:T(8,128)S(1)} %get-tuple-element.16), kind=kOutput, calls=%fused_computation.20 | convolution fusion | flops 986578944 | bytes 14427904 | tf_op jit(solution)/shard_map/ab,czby->czay/dot_general | solution.py:81
  111.2 8.3 %pad_maximum_fusion.2 = f32[2,2,16,32,1024]{4,3,2,1,0:T(8,128)} fusion(f32[1,2,16,32,1024]{4,3,2,1,0:T(8,128)} %stack_reshape.13, f32[1,2,16,32,1024]{4,3,2,1,0:T(8,128)} %stack_reshape.12), kind=kLoop, calls=%fused_computation.14 | loop fusion | flops 2097152 | bytes 16777216 | tf_op jit(solution)/shard_map/stack | solution.py:83
  119.6 26.6 %copy.65 = f32[2,2,16,32,1024]{3,2,1,0,4:T(8,128)} copy(f32[2,2,16,32,1024]{4,3,2,1,0:T(8,128)} %pad_maximum_fusion.2) | data formatting | bytes 16777216 | tf_op jit(solution)/shard_map/stack | solution.py:83
  146.1 20.5 %reshape.373 = f32[8,1,262144]{2,1,0:T(1,128)} reshape(f32[1024,2,2,16,32]{4,3,2,1,0:T(8,128)} %bitcast.192) | data formatting | bytes 16777216
  166.6 5.5 all-to-all-start
  187.9 150.7 %all-to-all-done = f32[8,1,262144]{2,1,0:T(1,128)} async-done(((f32[8,1,262144]{2,1,0:T(1,128)}), f32[8,1,262144]{2,1,0:T(1,128)}, u32[]{:S(2)}, u32[]{:S(2)}) %all-to-all-start) | async-done | bytes 8388640 | tf_op jit(solution)/shard_map/all_to_all | solution.py:83
  339.1 26.4 %reduce.6 = f32[8,262144]{1,0:T(8,128)} reduce(f32[8,1,262144]{2,1,0:T(1,128)} %all-to-all-done, f32[]{:T(128)} %broadcast.385), dimensions={1}, to_apply=%all_to_all.22.reduce_sub_computation | reduce | bytes 16777220 | tf_op jit(solution)/shard_map/all_to_all | solution.py:83
  365.5 25.3 %reshape.374 = f32[1024,2,2,16,32]{4,3,2,1,0:T(8,128)} reshape(f32[8,262144]{1,0:T(8,128)} %reduce.6) | data formatting | bytes 16777216
  390.7 18.4 %copy.97 = f32[2,2,16,32,8,128]{5,4,3,2,1,0:T(8,128)} copy(f32[2,2,16,32,8,128]{3,2,1,0,5,4:T(8,128)} %bitcast.193) | data formatting | bytes 16777216 | tf_op jit(solution)/shard_map/all_to_all | solution.py:83
  414.8 8.4 %fusion.18 = f32[2,32,128,128]{3,2,1,0:T(8,128)S(1)} fusion(f32[2,128,32,128]{3,2,1,0:T(8,128)S(1)} %bitcast.206, f32[128,128]{1,0:T(8,128)S(1)} %get-tuple-element.5), kind=kOutput, calls=%fused_computation.41 | convolution fusion | flops 1610612736 | bytes 8454144 | tf_op jit(solution)/shard_map/oi,cixy->coxy/dot_general | solution.py:86
  427.3 8.4 %fusion.16 = f32[2,32,128,128]{3,2,1,0:T(8,128)S(1)} fusion(f32[2,128,32,128]{3,2,1,0:T(8,128)S(1)} %bitcast.205, f32[128,128]{1,0:T(8,128)S(1)} %get-tuple-element.6), kind=kOutput, calls=%fused_computation.39 | convolution fusion | flops 1610612736 | bytes 8454144 | tf_op jit(solution)/shard_map/oi,cixy->coxy/dot_general | solution.py:86
  443.8 10.3 %copy.72 = f32[2,2,128,32,128]{4,3,1,0,2:T(8,128)} copy(f32[2,2,128,32,128]{2,4,3,1,0:T(8,128)} %pad_maximum_fusion.3) | data formatting | bytes 16777216 | tf_op jit(solution)/shard_map/stack | solution.py:89
  454.1 187.0 %all_to_all.30 = f32[2,2,128,32,128]{4,3,1,0,2:T(8,128)S(1)} all-to-all(f32[2,2,128,32,128]{4,3,1,0,2:T(8,128)} %copy.72), channel_id=1, replica_groups=mesh['view'=4,'slab'=8] {'slab'}, dimensions={2} | all-to-all | bytes 16777216 | tf_op jit(solution)/shard_map/all_to_all | solution.py:89
  641.1 8.1 copy.111
  670.6 5.3 fusion.33
  696.6 9.5 %fusion.68 = (f32[2,2,16,23,1024]{4,3,2,1,0:T(8,128)}, f32[2,2,16,23,1024]{4,3,2,1,0:T(8,128)S(1)}) fusion(f32[2,2,16,32,1024]{4,3,2,1,0:T(8,128)} %constant_dynamic-update-slice_fusion), kind=kLoop, calls=%fused_computation.165 | loop fusion | bytes 24117248 | tf_op jit(solution)/shard_map/slice | solution.py:18
  706.2 6.3 copy.75
  721.8 59.3 %collective-permute-done.2 = f32[2,2,16,23,1024]{4,2,3,1,0:T(8,128)S(1)} collective-permute-done((f32[2,2,16,23,1024]{4,2,3,1,0:T(8,128)S(1)}, f32[2,2,16,23,1024]{4,2,3,1,0:T(8,128)S(1)}, u32[]{:S(2)}, u32[]{:S(2)}) %collective-permute-start.2) | collective-permute-done | bytes 6029344 | tf_op jit(solution)/shard_map/ppermute | solution.py:20
  789.4 6.2 copy.78
  795.6 8.4 %pad_maximum_fusion = f32[2,2,16,78,1024]{4,3,2,1,0:T(8,128)S(1)} fusion(f32[2,2,16,23,1024]{4,3,2,1,0:T(8,128)} %copy.78, f32[2,2,16,32,1024]{4,3,2,1,0:T(8,128)} %constant_dynamic-update-slice_fusion, f32[2,2,16,23,1024]{4,3,2,1,0:T(8,128)S(1)} %copy.77), kind=kLoop, calls=%fused_computation | loop fusion | flops 10223616 | bytes 40894464 | tf_op jit(solution)/shard_map/concatenate | solution.py:22
  804.1 12.3 %fusion = f32[2,16,1024,32]{2,3,1,0:T(8,128)} fusion(f32[2,2,16,78,1024]{4,3,2,1,0:T(8,128)S(1)} %pad_maximum_fusion, f32[32,78]{1,0:T(8,128)S(1)} %copy-done.15), kind=kOutput, calls=%fused_computation.2 | convolution fusion | flops 981467136 | bytes 14696448 | tf_op jit(solution)/shard_map/ab,czby->czay/dot_general | solution.py:98
  816.4 14.9 %bitcast_multiply_fusion = f32[2,16,32,1024]{3,2,1,0:T(8,128)} fusion(f32[2,16,32,1024]{3,2,1,0:T(8,128)S(1)} %copy-done.1, f32[2,16,1024,32]{2,3,1,0:T(8,128)} %fusion, f32[2,2,16,78,1024]{4,3,2,1,0:T(8,128)S(1)} %pad_maximum_fusion, f32[32,78]{1,0:T(8,128)S(1)} %copy-done.14), kind=kOutput, calls=%fused_computation.36 | convolution fusion | flops 984612864 | bytes 23085056 | tf_op jit(solution)/shard_map/ab,czby->czay/dot_general | solution.py:98
  (100 shorter events, 167.4 us)
Async XLA Ops:
  5.5 8.3 copy-start.18
  5.5 9.0 %copy-start.16 = (f32[2,2,31]{2,1,0:T(2,128)S(1)}, f32[2,2,31]{2,1,0:T(2,128)}, u32[]{:S(2)}) copy-start(f32[2,2,31]{2,1,0:T(2,128)} %param.7) | copy-start | bytes 1492
  5.5 37.3 %collective-permute-start = (f32[2,16,23,1024]{3,1,2,0:T(8,128)S(1)}, f32[2,16,23,1024]{3,1,2,0:T(8,128)S(1)}, u32[]{:S(2)}, u32[]{:S(2)}) collective-permute-start(f32[2,16,23,1024]{3,1,2,0:T(8,128)S(1)} %copy.101), channel_id=1, source_target_pairs={{0,8},{8,16},{16,24},{1,9},{9,17},{17,25},{2,10},{10,18},{18,26},{... | collective-permute-start | bytes 9043976 | tf_op jit(solution)/shard_map/ppermute | solution.py:20
  11.8 37.2 %collective-permute-start.1 = (f32[2,16,23,1024]{3,1,2,0:T(8,128)S(1)}, f32[2,16,23,1024]{3,1,2,0:T(8,128)S(1)}, u32[]{:S(2)}, u32[]{:S(2)}) collective-permute-start(f32[2,16,23,1024]{3,1,2,0:T(8,128)S(1)} %copy.102), channel_id=1, source_target_pairs={{8,0},{16,8},{24,16},{9,1},{17,9},{25,17},{10,2},{18,10},{26,18},{... | collective-permute-start | bytes 9043976 | tf_op jit(solution)/shard_map/ppermute | solution.py:21
  44.6 6.2 copy-start
  50.7 11.1 %copy-start.4 = (f32[2,16,23,1024]{3,2,1,0:T(8,128)}, f32[2,16,23,1024]{3,2,1,0:T(8,128)S(1)}, u32[]{:S(2)}) copy-start(f32[2,16,23,1024]{3,2,1,0:T(8,128)S(1)} %copy.64) | copy-start | bytes 9043972
  166.6 172.0 %all-to-all-start = ((f32[8,1,262144]{2,1,0:T(1,128)}), f32[8,1,262144]{2,1,0:T(1,128)}, u32[]{:S(2)}, u32[]{:S(2)}) async-start(f32[8,1,262144]{2,1,0:T(1,128)} %reshape.373), calls=%async_computation | async-start | bytes 16777216 | tf_op jit(solution)/shard_map/all_to_all | solution.py:83
  176.6 7.5 copy-start.17
  414.8 8.4 %copy-start.7 = (bf16[1,2,128,32,128]{2,4,3,1,0:T(8,128)(2,1)S(1)}, bf16[1,2,128,32,128]{2,4,3,1,0:T(8,128)(2,1)}, u32[]{:S(2)}) copy-start(bf16[1,2,128,32,128]{2,4,3,1,0:T(8,128)(2,1)} %copy.100) | copy-start | bytes 6291460
  427.3 8.4 %copy-start.6 = (bf16[1,2,128,32,128]{2,4,3,1,0:T(8,128)(2,1)S(1)}, bf16[1,2,128,32,128]{2,4,3,1,0:T(8,128)(2,1)}, u32[]{:S(2)}) copy-start(bf16[1,2,128,32,128]{2,4,3,1,0:T(8,128)(2,1)} %copy.103) | copy-start | bytes 6291460
  649.2 4.5 copy-start.2
  649.2 4.5 copy-start.13
  653.7 3.6 copy-start.12
  657.3 3.4 copy-start.11
  665.7 4.9 copy-start.10
  670.6 5.4 copy-start.3
  670.6 5.4 copy-start.9
  676.0 3.4 copy-start.8
  689.5 4.9 copy-start.5
  712.4 68.7 %collective-permute-start.2 = (f32[2,2,16,23,1024]{4,2,3,1,0:T(8,128)S(1)}, f32[2,2,16,23,1024]{4,2,3,1,0:T(8,128)S(1)}, u32[]{:S(2)}, u32[]{:S(2)}) collective-permute-start(f32[2,2,16,23,1024]{4,2,3,1,0:T(8,128)S(1)} %copy.75), channel_id=1, source_target_pairs={{0,8},{8,16},{16,24},{1,9},{9,17},{17,25},{2,10},{10,18},{18,26},{... | collective-permute-start | bytes 18087944 | tf_op jit(solution)/shard_map/ppermute | solution.py:20
  719.9 69.5 %collective-permute-start.3 = (f32[2,2,16,23,1024]{4,2,3,1,0:T(8,128)S(1)}, f32[2,2,16,23,1024]{4,2,3,1,0:T(8,128)S(1)}, u32[]{:S(2)}, u32[]{:S(2)}) collective-permute-start(f32[2,2,16,23,1024]{4,2,3,1,0:T(8,128)S(1)} %copy.76), channel_id=1, source_target_pairs={{8,0},{16,8},{24,16},{9,1},{17,9},{25,17},{10,2},{18,10},{26,18},{... | collective-permute-start | bytes 18087944 | tf_op jit(solution)/shard_map/ppermute | solution.py:21
  795.6 8.4 %copy-start.15 = (f32[32,78]{1,0:T(8,128)S(1)}, f32[32,78]{1,0:T(8,128)}, u32[]{:S(2)}) copy-start(f32[32,78]{1,0:T(8,128)} %get-tuple-element.15) | copy-start | bytes 29956
  804.0 12.3 %copy-start.1 = (f32[2,16,32,1024]{3,2,1,0:T(8,128)S(1)}, f32[2,16,32,1024]{3,2,1,0:T(8,128)}, u32[]{:S(2)}) copy-start(f32[2,16,32,1024]{3,2,1,0:T(8,128)} %param.5) | copy-start | bytes 12582916
  804.1 12.3 %copy-start.14 = (f32[32,78]{1,0:T(8,128)S(1)}, f32[32,78]{1,0:T(8,128)}, u32[]{:S(2)}) copy-start(f32[32,78]{1,0:T(8,128)} %get-tuple-element.62) | copy-start | bytes 29956
where the time goes:
time: 839 us; the launch traced here: 831 us
  waiting for transfers between devices  232 us (28%)
  local copies, waits for them, and re-layouts  201 us (24%)
  blocking collectives  187 us (22%)
  matrix products  126 us (15%)
  other arithmetic  66.6 us (8%)
  starting transfers between devices  17.9 us (2%)
    all_to_all x1, blocking collectives, shards(): lax.all_to_all(jnp.stack(spread), 'slab', split_axis=2, concat_axis=4, ti...  187 us
    all_to_all x1, waiting for transfers between devices, shards(): lax.all_to_all(jnp.stack(blurred), 'slab', split_axis=4, concat_axis=2, t...  151 us
    ppermute x2, waiting for transfers between devices, with_halo(): before = lax.ppermute(last, axis, up)  71.8 us
    unnamed x47, local copies, waits for them, and re-layouts  65 us
    dot_general x12, matrix products, blocked_rows(): jnp.einsum('czxkj,ji->czxki', padded[:, :, :, shifted:shifted + blocks],...  49.3 us
    another operation x3, local copies, waits for them, and re-layouts, shards(): jnp.stack(blurred)  36.7 us
    dot_general x2, matrix products, shards(): jnp.einsum('ab,czby->czay', across, fringe[which], precision=HIGHEST)  27.2 us
    all_to_all x1, other arithmetic, shards(): lax.all_to_all(jnp.stack(blurred), 'slab', split_axis=4, concat_axis=2, t...  26.4 us
  transfers between devices with their start and end apart: 5, of which 5 were waited for; matrix products, arithmetic and copies ran while one was open for 5% of the time, Pallas kernels for 0%

commit v1 on v0

--- a/solution.py
+++ b/solution.py
@@ -80,7 +80,12 @@
         across = margin_matrix(along_x[which], offsets[which, 0], x_rows, HALO, False)
         sectioned = jnp.einsum("ab,czby->czay", across, widened, precision=HIGHEST)
         blurred.append(blocked_rows(sectioned, along_y[which], offsets[which, 1], YBLK, False))
-    columns = lax.all_to_all(jnp.stack(blurred), "slab", split_axis=4, concat_axis=2, tiled=True)
+    columns = jnp.concatenate(
+        lax.all_to_all(
+            jnp.stack(jnp.split(jnp.stack(blurred), lax.axis_size("slab"), axis=4)), "slab", 0, 0
+        ),
+        axis=2,
+    )
     spread = []
     for which in range(views_n):
         imaged = jnp.einsum("oi,cixy->coxy", axial[which], columns[which], precision=HIGHEST)

time: 839 us -> 726 us (0.87)
  local copies, waits for them, and re-layouts: 201 us -> 123 us
  other arithmetic: 66.6 us -> 31.5 us
    ppermute x2, waiting for transfers between devices: 71.8 us -> 2.54 us  [with_halo(): before = lax.ppermute(last, axis, up)]
    ppermute x2, waiting for transfers between devices: 9.2 us -> 74.2 us  [with_halo(): after = lax.ppermute(leading, axis, down)]
    unnamed x47 -> x43, local copies, waits for them, and re-layouts: 65 us -> 31.4 us
    another operation x3, local copies, waits for them, and re-layouts: 36.7 us -> 10.4 us  [shards(): jnp.stack(blurred)]
    all_to_all x1 -> x0, other arithmetic: 26.4 us -> none  [shards(): lax.all_to_all(jnp.stack(blurred), 'slab', split_axis=4, concat_axis=2, t...]
    all_to_all x2 -> x1, local copies, waits for them, and re-layouts: 18.9 us -> 4.37 us  [shards(): lax.all_to_all(jnp.stack(jnp.split(jnp.stack(blurred), lax.axis_size('sla...]
  transfers between devices with their start and end apart: 5 -> 5, of which waited for: 5 -> 5; matrix products, arithmetic and copies ran while one was open for 5% -> 6% of each run, Pallas kernels for 0% -> 0%
where the time goes in v1:
time: 726 us; the launch traced here: 719 us
  waiting for transfers between devices  230 us (32%)
  blocking collectives  187 us (26%)
  matrix products  128 us (18%)
  local copies, waits for them, and re-layouts  123 us (17%)
  other arithmetic  31.5 us (4%)
  starting transfers between devices  17.7 us (2%)
    all_to_all x1, blocking collectives, shards(): lax.all_to_all(jnp.stack(spread), 'slab', split_axis=2, concat_axis=4, ti...  187 us
    all_to_all x1, waiting for transfers between devices, shards(): lax.all_to_all(jnp.stack(jnp.split(jnp.stack(blurred), lax.axis_size('sla...  154 us
    ppermute x2, waiting for transfers between devices, with_halo(): after = lax.ppermute(leading, axis, down)  74.2 us
    dot_general x12, matrix products, blocked_rows(): jnp.einsum('czxkj,ji->czxki', padded[:, :, :, shifted:shifted + blocks],...  53.5 us
    unnamed x43, local copies, waits for them, and re-layouts  31.4 us
    dot_general x2, matrix products, shards(): jnp.einsum('ab,czby->czay', across, fringe[which], precision=HIGHEST)  27.2 us
    dot_general x2, matrix products, shards(): sectioned = jnp.einsum('ab,czby->czay', across, widened, precision=HIGHEST)  22.2 us
    dot_general x2, matrix products, shards(): jnp.einsum('oi,cixy->coxy', axial[which], columns[which], precision=HIGHEST)  16.8 us
  transfers between devices with their start and end apart: 5, of which 5 were waited for; matrix products, arithmetic and copies ran while one was open for 6% of the time, Pallas kernels for 0%

profile of v1, /device:TPU:1, one launch (start us, length us, event | category | flops | bytes accessed | tf_op | source)
XLA Modules:
  0.0 718.7 jit_solution(4616385753718733877)
XLA Ops:
  29.6 14.0 %collective-permute-done.1 = f32[2,16,23,1024]{3,1,2,0:T(8,128)S(1)} collective-permute-done((f32[2,16,23,1024]{3,1,2,0:T(8,128)S(1)}, f32[2,16,23,1024]{3,1,2,0:T(8,128)S(1)}, u32[]{:S(2)}, u32[]{:S(2)}) %collective-permute-start.1) | collective-permute-done | bytes 3014688 | tf_op jit(solution)/shard_map/ppermute | solution.py:21
  48.3 11.1 %fusion.2 = f32[2,16,1024,32]{2,3,1,0:T(8,128)S(1)} fusion(f32[2,16,23,1024]{3,2,1,0:T(8,128)S(1)} %copy.40, f32[2,16,32,1024]{3,2,1,0:T(8,128)S(1)} %copy-done, f32[2,16,23,1024]{3,2,1,0:T(8,128)S(1)} %copy.39, f32[32,78]{1,0:T(8,128)S(1)} %get-tuple-element.16), kind=kOutput, calls=%fused_computation.20 | convolution fusion | flops 986578944 | bytes 14427904 | tf_op jit(solution)/shard_map/ab,czby->czay/dot_general | solution.py:81
  59.4 11.1 %fusion.3 = f32[2,16,1024,32]{2,3,1,0:T(8,128)S(1)} fusion(f32[2,16,23,1024]{3,2,1,0:T(8,128)S(1)} %copy.40, f32[2,16,32,1024]{3,2,1,0:T(8,128)S(1)} %copy-done, f32[2,16,23,1024]{3,2,1,0:T(8,128)S(1)} %copy.39, f32[32,78]{1,0:T(8,128)S(1)} %get-tuple-element.61), kind=kOutput, calls=%fused_computation.21 | convolution fusion | flops 986578944 | bytes 14427904 | tf_op jit(solution)/shard_map/ab,czby->czay/dot_general | solution.py:81
  81.4 4.9 add_add_fusion.2
  91.2 5.8 fusion.53
  100.4 4.9 add_add_fusion.3
  123.5 5.5 all-to-all-start
  144.9 153.7 %all-to-all-done = f32[8,2,2,16,32,128]{5,4,3,2,1,0:T(8,128)} async-done(((f32[8,2,2,16,32,128]{5,4,3,2,1,0:T(8,128)}), f32[8,2,2,16,32,128]{5,4,3,2,1,0:T(8,128)}, u32[]{:S(2)}, u32[]{:S(2)}) %all-to-all-start) | async-done | bytes 8388640 | tf_op jit(solution)/shard_map/all_to_all | solution.py:84
  304.5 8.4 %fusion.18 = f32[2,32,128,128]{3,2,1,0:T(8,128)S(1)} fusion(f32[2,128,32,128]{3,2,1,0:T(8,128)S(1)} %bitcast.237, f32[128,128]{1,0:T(8,128)S(1)} %get-tuple-element.5), kind=kOutput, calls=%fused_computation.41 | convolution fusion | flops 1610612736 | bytes 8454144 | tf_op jit(solution)/shard_map/oi,cixy->coxy/dot_general | solution.py:91
  317.3 8.4 %fusion.16 = f32[2,32,128,128]{3,2,1,0:T(8,128)S(1)} fusion(f32[2,128,32,128]{3,2,1,0:T(8,128)S(1)} %bitcast.234, f32[128,128]{1,0:T(8,128)S(1)} %get-tuple-element.6), kind=kOutput, calls=%fused_computation.39 | convolution fusion | flops 1610612736 | bytes 8454144 | tf_op jit(solution)/shard_map/oi,cixy->coxy/dot_general | solution.py:91
  333.5 10.3 %copy.45 = f32[2,2,128,32,128]{4,3,1,0,2:T(8,128)} copy(f32[2,2,128,32,128]{2,4,3,1,0:T(8,128)} %pad_maximum_fusion.2) | data formatting | bytes 16777216 | tf_op jit(solution)/shard_map/stack | solution.py:94
  343.8 187.0 %all_to_all.20 = f32[2,2,128,32,128]{4,3,1,0,2:T(8,128)S(1)} all-to-all(f32[2,2,128,32,128]{4,3,1,0,2:T(8,128)} %copy.45), channel_id=1, replica_groups=mesh['view'=4,'slab'=8] {'slab'}, dimensions={2} | all-to-all | bytes 16777216 | tf_op jit(solution)/shard_map/all_to_all | solution.py:94
  530.8 8.1 %copy.84 = f32[2,2,8,16,32,128]{5,2,4,3,1,0:T(8,128)S(1)} copy(f32[2,2,8,16,32,128]{5,4,1,0,3,2:T(8,128)S(1)} %bitcast.233) | data formatting | bytes 16777216 | tf_op jit(solution)/shard_map/all_to_all | solution.py:94
  541.7 5.1 fusion.41
  553.6 4.9 add_add_fusion
  563.4 5.4 fusion.8
  568.9 5.3 add_add_fusion.1
  586.3 9.5 %fusion.76 = (f32[2,2,16,23,1024]{4,3,2,1,0:T(8,128)S(1)}, f32[2,2,16,23,1024]{4,3,2,1,0:T(8,128)}) fusion(f32[2,2,16,32,1024]{4,3,2,1,0:T(8,128)} %constant_dynamic-update-slice_fusion.2), kind=kLoop, calls=%fused_computation.183 | loop fusion | bytes 24117248 | tf_op jit(solution)/shard_map/slice | solution.py:18
  595.7 6.3 copy.49
  611.3 60.2 %collective-permute-done.3 = f32[2,2,16,23,1024]{4,2,3,1,0:T(8,128)S(1)} collective-permute-done((f32[2,2,16,23,1024]{4,2,3,1,0:T(8,128)S(1)}, f32[2,2,16,23,1024]{4,2,3,1,0:T(8,128)S(1)}, u32[]{:S(2)}, u32[]{:S(2)}) %collective-permute-start.3) | collective-permute-done | bytes 6029344 | tf_op jit(solution)/shard_map/ppermute | solution.py:21
  676.4 6.2 copy.50
  682.6 8.6 %pad_maximum_fusion = f32[2,2,16,78,1024]{4,3,2,1,0:T(8,128)S(1)} fusion(f32[2,2,16,23,1024]{4,3,2,1,0:T(8,128)S(1)} %copy.51, f32[2,2,16,32,1024]{4,3,2,1,0:T(8,128)} %constant_dynamic-update-slice_fusion.2, f32[2,2,16,23,1024]{4,3,2,1,0:T(8,128)} %copy.50), kind=kLoop, calls=%fused_computation | loop fusion | flops 10223616 | bytes 40894464 | tf_op jit(solution)/shard_map/concatenate | solution.py:22
  691.3 12.3 %fusion = f32[2,16,1024,32]{2,3,1,0:T(8,128)} fusion(f32[2,2,16,78,1024]{4,3,2,1,0:T(8,128)S(1)} %pad_maximum_fusion, f32[32,78]{1,0:T(8,128)S(1)} %copy-done.10), kind=kOutput, calls=%fused_computation.2 | convolution fusion | flops 981467136 | bytes 14696448 | tf_op jit(solution)/shard_map/ab,czby->czay/dot_general | solution.py:103
  703.5 14.9 %bitcast_multiply_fusion = f32[2,16,32,1024]{3,2,1,0:T(8,128)} fusion(f32[2,16,32,1024]{3,2,1,0:T(8,128)S(1)} %copy-done.1, f32[2,16,1024,32]{2,3,1,0:T(8,128)} %fusion, f32[2,2,16,78,1024]{4,3,2,1,0:T(8,128)S(1)} %pad_maximum_fusion, f32[32,78]{1,0:T(8,128)S(1)} %copy-done.9), kind=kOutput, calls=%fused_computation.36 | convolution fusion | flops 984612864 | bytes 23085056 | tf_op jit(solution)/shard_map/ab,czby->czay/dot_general | solution.py:103
  (92 shorter events, 145.9 us)
Async XLA Ops:
  5.5 8.3 %copy-start.13 = (s32[2,2]{1,0:T(2,128)S(1)}, s32[2,2]{1,0:T(2,128)}, u32[]{:S(2)}) copy-start(s32[2,2]{1,0:T(2,128)} %param.9) | copy-start | bytes 52
  5.5 9.0 %copy-start.11 = (f32[2,2,31]{2,1,0:T(2,128)S(1)}, f32[2,2,31]{2,1,0:T(2,128)}, u32[]{:S(2)}) copy-start(f32[2,2,31]{2,1,0:T(2,128)} %param.7) | copy-start | bytes 1492
  5.5 38.1 %collective-permute-start.1 = (f32[2,16,23,1024]{3,1,2,0:T(8,128)S(1)}, f32[2,16,23,1024]{3,1,2,0:T(8,128)S(1)}, u32[]{:S(2)}, u32[]{:S(2)}) collective-permute-start(f32[2,16,23,1024]{3,1,2,0:T(8,128)S(1)} %copy.74), channel_id=1, source_target_pairs={{8,0},{16,8},{24,16},{9,1},{17,9},{25,17},{10,2},{18,10},{26,18},{... | collective-permute-start | bytes 9043976 | tf_op jit(solution)/shard_map/ppermute | solution.py:21
  9.2 37.3 %collective-permute-start = (f32[2,16,23,1024]{3,1,2,0:T(8,128)S(1)}, f32[2,16,23,1024]{3,1,2,0:T(8,128)S(1)}, u32[]{:S(2)}, u32[]{:S(2)}) collective-permute-start(f32[2,16,23,1024]{3,1,2,0:T(8,128)S(1)} %copy.73), channel_id=1, source_target_pairs={{0,8},{8,16},{16,24},{1,9},{9,17},{17,25},{2,10},{10,18},{18,26},{... | collective-permute-start | bytes 9043976 | tf_op jit(solution)/shard_map/ppermute | solution.py:20
  45.3 2.9 copy-start
  91.2 5.8 copy-start.2
  110.3 3.4 copy-start.4
  123.5 175.0 %all-to-all-start = ((f32[8,2,2,16,32,128]{5,4,3,2,1,0:T(8,128)}), f32[8,2,2,16,32,128]{5,4,3,2,1,0:T(8,128)}, u32[]{:S(2)}, u32[]{:S(2)}) async-start(f32[8,2,2,16,32,128]{5,4,3,2,1,0:T(8,128)} %fusion.28), calls=%async_computation | async-start | bytes 16777216 | tf_op jit(solution)/shard_map/all_to_all | solution.py:84
  133.5 7.4 %copy-start.12 = (f32[2,127]{1,0:T(2,128)S(1)}, f32[2,127]{1,0:T(2,128)}, u32[]{:S(2)}) copy-start(f32[2,127]{1,0:T(2,128)} %param.8) | copy-start | bytes 3052
  304.5 8.4 %copy-start.8 = (bf16[1,2,128,32,128]{2,4,3,1,0:T(8,128)(2,1)S(1)}, bf16[1,2,128,32,128]{2,4,3,1,0:T(8,128)(2,1)}, u32[]{:S(2)}) copy-start(bf16[1,2,128,32,128]{2,4,3,1,0:T(8,128)(2,1)} %copy.72) | copy-start | bytes 6291460
  317.3 8.4 %copy-start.7 = (bf16[1,2,128,32,128]{2,4,3,1,0:T(8,128)(2,1)S(1)}, bf16[1,2,128,32,128]{2,4,3,1,0:T(8,128)(2,1)}, u32[]{:S(2)}) copy-start(bf16[1,2,128,32,128]{2,4,3,1,0:T(8,128)(2,1)} %copy.75) | copy-start | bytes 6291460
  563.4 5.4 copy-start.3
  563.4 5.4 copy-start.6
  579.1 4.9 copy-start.5
  602.0 69.5 %collective-permute-start.3 = (f32[2,2,16,23,1024]{4,2,3,1,0:T(8,128)S(1)}, f32[2,2,16,23,1024]{4,2,3,1,0:T(8,128)S(1)}, u32[]{:S(2)}, u32[]{:S(2)}) collective-permute-start(f32[2,2,16,23,1024]{4,2,3,1,0:T(8,128)S(1)} %copy.49), channel_id=1, source_target_pairs={{8,0},{16,8},{24,16},{9,1},{17,9},{25,17},{10,2},{18,10},{26,18},{... | collective-permute-start | bytes 18087944 | tf_op jit(solution)/shard_map/ppermute | solution.py:21
  608.3 68.0 %collective-permute-start.2 = (f32[2,2,16,23,1024]{4,2,3,1,0:T(8,128)S(1)}, f32[2,2,16,23,1024]{4,2,3,1,0:T(8,128)S(1)}, u32[]{:S(2)}, u32[]{:S(2)}) collective-permute-start(f32[2,2,16,23,1024]{4,2,3,1,0:T(8,128)S(1)} %copy.48), channel_id=1, source_target_pairs={{0,8},{8,16},{16,24},{1,9},{9,17},{17,25},{2,10},{10,18},{18,26},{... | collective-permute-start | bytes 18087944 | tf_op jit(solution)/shard_map/ppermute | solution.py:20
  682.6 8.7 %copy-start.10 = (f32[32,78]{1,0:T(8,128)S(1)}, f32[32,78]{1,0:T(8,128)}, u32[]{:S(2)}) copy-start(f32[32,78]{1,0:T(8,128)} %get-tuple-element.15) | copy-start | bytes 29956
  691.2 12.3 %copy-start.1 = (f32[2,16,32,1024]{3,2,1,0:T(8,128)S(1)}, f32[2,16,32,1024]{3,2,1,0:T(8,128)}, u32[]{:S(2)}) copy-start(f32[2,16,32,1024]{3,2,1,0:T(8,128)} %param.5) | copy-start | bytes 12582916
  691.2 12.3 %copy-start.9 = (f32[32,78]{1,0:T(8,128)S(1)}, f32[32,78]{1,0:T(8,128)}, u32[]{:S(2)}) copy-start(f32[32,78]{1,0:T(8,128)} %get-tuple-element.62) | copy-start | bytes 29956
